TPU v7x, 256 devices: a whole 4x4x8 slice. The times are simulated.
256 devices in a mesh: row: 16 (over z, core), col: 4 (over x), depth: 4 (over y).
Axes of the slice: x: 4, y: 4, z: 8, core: 2. Of those that a mesh axis runs over, the one named last changes fastest.
Arguments:
- residual: float32 [2048, 4096], P(('row', 'depth'), 'col'), may hold values from -4 to 4
- amplitudes: float32 [2048, 65536], P('col', ('row', 'depth')), may hold values from -6 to 6
- integrals: float32 [65536, 4096], P(('row', 'depth'), 'col'), may hold values from -0.0390625 to 0.0390625
- t2_mask: int32 [16, 512], P('col', ('row', 'depth')), may hold values from 0 to 1, as said below
- v_mask: int32 [512, 32], P(('row', 'depth'), 'col'), may hold values from 0 to 1, as said below
Outputs:
- updated: float32 [2048, 4096], P(('row', 'depth'), 'col')
Inputs may be any that keep to these rules, and one draw needn't show every extreme that they name: `t2_mask`: each entry flags one 128 x 128 amplitude tile as kept (1) or zero (0). `v_mask`: each entry flags one 128 x 128 integral tile as kept (1) or zero (0).
All inputs are finite; a program needn't handle non-finite values.
Results may differ from a plain program's by a relative error of at most 0.0001.
Values sent between devices are 32-bit elements; how exact they have to be, the bound alone decides.
A program may use at most 64 MiB of HBM per device.

v0:
```python
import jax
import jax.numpy as jnp
from jax import lax
from jax.sharding import PartitionSpec as P

TILE = 128


def apply_flags(matrix, tile_flags):
    tile_rows, tile_cols = tile_flags.shape
    tiled = (
        matrix.reshape(tile_rows, TILE, tile_cols, TILE)
        * tile_flags.astype(jnp.float32)[:, None, :, None]
    )
    return tiled.reshape(matrix.shape)


def per_device(residual, amplitudes, integrals, t2_mask, v_mask):
    amplitude_kept = apply_flags(amplitudes, t2_mask)
    integral_kept = apply_flags(integrals, v_mask)
    panels = lax.all_gather(amplitude_kept, "col", axis=0, tiled=True)
    summed = lax.psum_scatter(
        jnp.dot(
            panels,
            integral_kept,
            precision=lax.Precision.HIGHEST,
            preferred_element_type=jnp.float32,
        ),
        ("row", "depth"),
        scatter_dimension=0,
        tiled=True,
    )
    return residual + summed


def solution(mesh):
    in_specs = (
        P(("row", "depth"), "col"),
        P("col", ("row", "depth")),
        P(("row", "depth"), "col"),
        P("col", ("row", "depth")),
        P(("row", "depth"), "col"),
    )
    out_specs = P(("row", "depth"), "col")
    return jax.shard_map(
        per_device, mesh=mesh, in_specs=in_specs, out_specs=out_specs, check_vma=False
    )
```

profile of v0, /device:TPU:4, one launch (start us, length us, event | category | flops | bytes accessed | tf_op | source)
XLA Modules:
  0.0 295.0 jit_solution(5104896567255951643)
XLA Ops:
  6.5 0.0 all-gather.2.cloned.1.call-start
  6.5 0.7 convert_element_type.6
  7.2 0.2 mul.22
  7.4 0.0 copy-start.1
  7.4 3.7 %bitcast_multiply_fusion.2 = f32[512,1024]{1,0:T(8,128)} fusion(f32[512,1024]{1,0:T(8,128)} %param.6, f32[64,8,8,128]{3,2,1,0:T(8,128)S(1)} %bitcast.10), kind=kLoop, calls=%fused_computation.3 | loop fusion | flops 524288 | bytes 6291456 | tf_op jit(solution)/shard_map/mul | solution.py:12
  11.1 0.0 all-gather.2.cloned.1.call-update
  11.1 0.0 reduce-scatter.2.cloned.1.call-start
  11.2 0.0 copy-done.1
  11.2 88.4 %all-gather.2.cloned.1.call-done = f32[2048,1024]{1,0:T(8,128)} async-done(((f32[512,1024]{1,0:T(8,128)}), f32[2048,1024]{1,0:T(8,128)}) %all-gather.2.cloned.1.call-update) | async-done | bytes 8388624 | tf_op jit(solution)/shard_map/all_gather | solution.py:21
  99.6 0.0 copy-start.2
  99.6 0.3 mul.25
  99.9 1.8 copy-done.2
  101.8 32.0 %fusion = f32[2048,1024]{1,0:T(8,128)} fusion(f32[2048,1024]{1,0:T(8,128)} %all-gather.2.cloned.1.call-done, f32[1024,1024]{1,0:T(8,128)S(1)} %copy-done.2, f32[128,8,8,128]{3,2,1,0:T(8,128)S(1)} %bitcast.11), kind=kOutput, calls=%fused_computation.1 | convolution fusion | flops 25770852352 | bytes 25165824 | tf_op jit(solution)/shard_map/dot_general | solution.py:23
  133.7 0.0 copy-start
  133.7 0.0 reduce-scatter.2.cloned.1.call-update
  133.8 152.9 %reduce-scatter.2.cloned.1.call-done = f32[32,1024]{1,0:T(8,128)} async-done(((f32[2048,1024]{1,0:T(8,128)}), f32[32,1024]{1,0:T(8,128)}) %reduce-scatter.2.cloned.1.call-update) | async-done | bytes 131088 | tf_op jit(solution)/shard_map/reduce_scatter | solution.py:22
  286.6 0.0 copy-done
  286.6 1.6 add.5
  (1 shorter events, 0.0 us)
Async XLA Ops:
  6.5 93.0 %all-gather.2.cloned.1.call-start = ((), (), s32[]{:S(2)}) async-start(), calls=%async_computation.1 | async-start | bytes 10485760 | tf_op jit(solution)/shard_map/all_gather | solution.py:21
  7.4 3.8 %copy-start.1 = (s32[8,8]{1,0:T(8,128)S(1)}, s32[8,8]{1,0:T(8,128)}, u32[]{:S(2)}) copy-start(s32[8,8]{1,0:T(8,128)} %param.9) | copy-start | bytes 772
  11.1 275.5 %reduce-scatter.2.cloned.1.call-start = ((), (), s32[]{:S(2)}) async-start(), calls=%async_computation.2 | async-start | bytes 8519680 | tf_op jit(solution)/shard_map/reduce_scatter | solution.py:22
  99.6 2.2 copy-start.2
  133.7 152.9 %copy-start = (f32[32,1024]{1,0:T(8,128)S(1)}, f32[32,1024]{1,0:T(8,128)}, u32[]{:S(2)}) copy-start(f32[32,1024]{1,0:T(8,128)} %param.5) | copy-start | bytes 393220
Sparse Core Ops, SparseCore 0:
  11.3 88.2 all-gather.1
  133.9 152.6 reduce-scatter.1
where the time goes:
time: 295 us
  waiting for transfers between devices  241 us (82%)
  matrix products  32 us (11%)
  between operations  13.4 us (5%)
  other arithmetic  5.93 us (2%)
    reduce_scatter x1, waiting for transfers between devices, per_device(): lax.psum_scatter(jnp.dot(panels, integral_kept, precision=lax.Precision.H...  153 us
    all_gather x1, waiting for transfers between devices, per_device(): panels = lax.all_gather(amplitude_kept, 'col', axis=0, tiled=True)  88.4 us
    dot_general x1, matrix products, per_device(): jnp.dot(panels, integral_kept, precision=lax.Precision.HIGHEST, preferred...  32 us
  transfers between devices with their start and end apart: 2, of which 2 were waited for; matrix products, arithmetic and copies ran while one was open for 0% of the time, Pallas kernels for 0%

commit v1 on v0

--- a/solution.py
+++ b/solution.py
@@ -18,7 +18,10 @@
 def per_device(residual, amplitudes, integrals, t2_mask, v_mask):
     amplitude_kept = apply_flags(amplitudes, t2_mask)
     integral_kept = apply_flags(integrals, v_mask)
-    panels = lax.all_gather(amplitude_kept, "col", axis=0, tiled=True)
+    write_sector = lambda buf: jnp.concatenate(
+        lax.all_to_all(jnp.stack([buf for _ in range(lax.axis_size("col"))]), "col", 0, 0), 0
+    )
+    panels = write_sector(amplitude_kept)
     summed = lax.psum_scatter(
         jnp.dot(
             panels,

time: 295 us -> 309 us (1.047)
  starting transfers between devices: 0.04 us -> 7.98 us
  local copies, waits for them, and re-layouts: 2.39 us -> 6.67 us
    all_to_all x0 -> x1, waiting for transfers between devices: none -> 89.1 us  [per_device(): lax.all_to_all(jnp.stack([buf for _ in range(lax.axis_size('col'))]), 'co...]
    all_gather x1 -> x0, waiting for transfers between devices: 88.4 us -> none  [per_device(): panels = lax.all_gather(amplitude_kept, 'col', axis=0, tiled=True)]
    all_to_all x0 -> x1, starting transfers between devices: none -> 7.97 us  [per_device(): lax.all_to_all(jnp.stack([buf for _ in range(lax.axis_size('col'))]), 'co...]
    another operation x0 -> x1, local copies, waits for them, and re-layouts: none -> 4.28 us  [per_device(): jnp.stack([buf for _ in range(lax.axis_size('col'))])]
where the time goes in v1:
time: 309 us
  waiting for transfers between devices  244 us (79%)
  matrix products  32 us (10%)
  between operations  13.4 us (4%)
  starting transfers between devices  7.98 us (3%)
  local copies, waits for them, and re-layouts  6.67 us (2%)
  other arithmetic  4.57 us (1%)
    reduce_scatter x1, waiting for transfers between devices, per_device(): lax.psum_scatter(jnp.dot(panels, integral_kept, precision=lax.Precision.H...  155 us
    all_to_all x1, waiting for transfers between devices, per_device(): lax.all_to_all(jnp.stack([buf for _ in range(lax.axis_size('col'))]), 'co...  89.1 us
    dot_general x1, matrix products, per_device(): jnp.dot(panels, integral_kept, precision=lax.Precision.HIGHEST, preferred...  32 us
    all_to_all x1, starting transfers between devices, per_device(): lax.all_to_all(jnp.stack([buf for _ in range(lax.axis_size('col'))]), 'co...  7.97 us
  transfers between devices with their start and end apart: 2, of which 2 were waited for; matrix products, arithmetic and copies ran while one was open for 0% of the time, Pallas kernels for 0%

profile of v1, /device:TPU:4, one launch (start us, length us, event | category | flops | bytes accessed | tf_op | source)
XLA Modules:
  0.0 309.1 jit_solution(15325275598445132829)
XLA Ops:
  6.5 0.7 convert_element_type.6
  7.2 0.2 mul.23
  7.4 2.3 bitcast_multiply_fusion.2
  9.7 4.3 %stack.3 = f32[4,512,1024]{2,1,0:T(8,128)} broadcast(f32[512,1024]{1,0:T(8,128)S(1)} %bitcast_multiply_fusion.2), dimensions={1,2} | broadcast | bytes 10485760 | tf_op jit(solution)/shard_map/stack | solution.py:22
  14.0 0.0 copy-start.1
  14.0 8.0 %all-to-all-start = ((f32[4,512,1024]{2,1,0:T(8,128)}), f32[4,512,1024]{2,1,0:T(8,128)}, u32[]{:S(2)}, u32[]{:S(2)}) async-start(f32[4,512,1024]{2,1,0:T(8,128)} %stack.3), calls=%async_computation | async-start | bytes 16777216 | tf_op jit(solution)/shard_map/all_to_all | solution.py:22
  22.0 0.0 reduce-scatter.2.cloned.1.call-start
  22.0 0.0 copy-done.1
  22.0 89.1 %all-to-all-done = f32[4,512,1024]{2,1,0:T(8,128)} async-done(((f32[4,512,1024]{2,1,0:T(8,128)}), f32[4,512,1024]{2,1,0:T(8,128)}, u32[]{:S(2)}, u32[]{:S(2)}) %all-to-all-start) | async-done | bytes 8388640 | tf_op jit(solution)/shard_map/all_to_all | solution.py:22
  111.1 0.0 copy-start.2
  111.1 0.3 mul.26
  111.5 1.8 copy-done.2
  113.3 32.0 %fusion = f32[2048,1024]{1,0:T(8,128)} fusion(f32[2048,1024]{1,0:T(8,128)} %bitcast, f32[1024,1024]{1,0:T(8,128)S(1)} %copy-done.2, f32[128,8,8,128]{3,2,1,0:T(8,128)S(1)} %bitcast.12), kind=kOutput, calls=%fused_computation.1 | convolution fusion | flops 25770852352 | bytes 25165824 | tf_op jit(solution)/shard_map/dot_general | solution.py:26
  145.3 0.0 copy-start
  145.3 0.0 reduce-scatter.2.cloned.1.call-update
  145.3 155.3 %reduce-scatter.2.cloned.1.call-done = f32[32,1024]{1,0:T(8,128)} async-done(((f32[2048,1024]{1,0:T(8,128)}), f32[32,1024]{1,0:T(8,128)}) %reduce-scatter.2.cloned.1.call-update) | async-done | bytes 131088 | tf_op jit(solution)/shard_map/reduce_scatter | solution.py:25
  300.6 0.0 copy-done
  300.6 1.6 add.5
  (1 shorter events, 0.0 us)
Async XLA Ops:
  14.0 8.0 %copy-start.1 = (s32[8,8]{1,0:T(8,128)S(1)}, s32[8,8]{1,0:T(8,128)}, u32[]{:S(2)}) copy-start(s32[8,8]{1,0:T(8,128)} %param.9) | copy-start | bytes 772
  14.0 97.1 %all-to-all-start = ((f32[4,512,1024]{2,1,0:T(8,128)}), f32[4,512,1024]{2,1,0:T(8,128)}, u32[]{:S(2)}, u32[]{:S(2)}) async-start(f32[4,512,1024]{2,1,0:T(8,128)} %stack.3), calls=%async_computation | async-start | bytes 16777216 | tf_op jit(solution)/shard_map/all_to_all | solution.py:22
  22.0 278.6 %reduce-scatter.2.cloned.1.call-start = ((), (), s32[]{:S(2)}) async-start(), calls=%async_computation.2 | async-start | bytes 8519680 | tf_op jit(solution)/shard_map/reduce_scatter | solution.py:25
  111.1 2.2 copy-start.2
  145.3 155.3 %copy-start = (f32[32,1024]{1,0:T(8,128)S(1)}, f32[32,1024]{1,0:T(8,128)}, u32[]{:S(2)}) copy-start(f32[32,1024]{1,0:T(8,128)} %param.5) | copy-start | bytes 393220
Sparse Core Ops, SparseCore 0:
  145.4 155.1 reduce-scatter.1
